TPU v7x, 128 devices: a whole 4x4x4 slice. The times are simulated.
128 devices in a mesh: tiles: 64 (over x, y, z), rows: 2 (over core).
Axes of the slice: x: 4, y: 4, z: 4, core: 2. Of those that a mesh axis runs over, the one named last changes fastest.
Arguments:
- frames: bfloat16 [64, 2, 64, 128, 256], P('tiles', None, None, 'rows'), may hold values from -6 to 6
- feat_weight: bfloat16 [9, 128, 64], replicated, may hold values from -0.25 to 0.25
- feat_bias: float32 [128], replicated, may hold values from -3 to 3
- send_rows: int32 [64, 2, 3, 2, 32], P('tiles', 'rows'), may hold values from 0 to 64, as said below
- recv_slots: int32 [64, 2, 64, 2], P('tiles', 'rows'), may hold values from 0 to 191, as said below
- blend: float32 [64, 2, 64, 2], P('tiles', 'rows'), may hold values from 0.2 to 0.8
- corr_weight: bfloat16 [256, 81], replicated, may hold values from -0.625 to 0.625
- corr_bias: float32 [256], replicated, may hold values from -4 to 4
- mid_weight: bfloat16 [9, 192, 256], replicated, may hold values from -0.125 to 0.125
- mid_bias: float32 [192], replicated, may hold values from -3 to 3
- flow_weight: bfloat16 [2, 192], replicated, may hold values from -0.4375 to 0.4375
- flow_bias: float32 [2], replicated, may hold values from -4 to 4
Outputs:
- flow: float32 [64, 2, 64, 128], P('tiles', None, 'rows')
Inputs may be any that keep to these rules, and one draw needn't show every extreme that they name: `send_rows`: the lists come from the intersections of a ground band with the bands of its own and the two neighbouring chips. Frame f's feature row y of a band is numbered f * 32 + y; 64 marks an empty slot. What one band sends to another is one contiguous run of rows of one frame, in order, from slot 0, followed by empty slots. `recv_slots`: Both entries of a ground row are slots c and c + 1 of the same window. Each frame's ground rows of a band split into two contiguous runs, each served by one sender; every band reads from 4 of its 6 windows, which ones drawn per band. In every band one sender fills all 32 of its slots.
All inputs are finite; a program needn't handle non-finite values.
Results may differ from a plain program's by a relative error of at most 0.0059.
Values may be sent and summed in bfloat16 or wider, within the bound.
A program may use at most 192 MiB of HBM per device.

v0:
```python
import functools

import jax
import jax.numpy as jnp
import numpy as np
from jax import lax
from jax.experimental import pallas as pl
from jax.experimental.pallas import tpu as pltpu
from jax.sharding import PartitionSpec as P

BF16 = jnp.bfloat16
F32 = jnp.float32
MESH = pl.DeviceIdType.MESH

CIN = 64
CH = 128
HID = 256
MID = 192
WIDTH = 128
BAND = 32
GROUP = 8
CHUNKS = 2 * BAND // GROUP
SPAN = 9
NT = (((1,), (1,)), ((), ()))


def lane_of(offset):
    step_row, step_col = offset // SPAN, offset % SPAN
    return WIDTH * (step_row // 5) + 24 * (step_row % 5) + 7 + 2 * step_col


def column_picks():
    picks = np.zeros((2 * WIDTH, 3 * WIDTH), np.float32)
    for tap in range(3):
        for column in range(WIDTH):
            source = 2 * column - 1 + tap
            if source >= 0:
                picks[source, tap * WIDTH + column] = 1.0
    return picks


def offset_lanes():
    lanes = np.zeros((2 * WIDTH, SPAN * SPAN), np.float32)
    for offset in range(SPAN * SPAN):
        lanes[lane_of(offset), offset] = 1.0
    return lanes


def kernel(
    tiles,
    frames,
    picks,
    conv_w,
    feat_b,
    sent,
    slots,
    blend,
    lanes,
    corr_w,
    corr_b,
    mid_w,
    mid_b,
    flow_w,
    flow_b,
    out,
    xin,
    split,
    taps,
    bias_t,
    rows,
    table_v,
    table_s,
    g0,
    g1,
    keep,
    corr_k,
    hid,
    in_sem,
    halo_send,
    halo_recv,
    row_send,
    row_recv,
    table_send,
    table_recv,
    edge_send,
    edge_recv,
    local_sem,
):
    t = lax.axis_index("tiles")
    r = lax.axis_index("rows")
    right, left = lax.rem(t + 1, tiles), lax.rem(t + tiles - 1, tiles)
    other = 1 - r

    order = [(f, g) for f in range(2) for g in (3, 2, 1, 0)]
    loads = {}
    for f, g in order:
        loads[f, g] = pltpu.make_async_copy(
            frames.at[0, f, :, pl.ds(16 * g, 16), :], xin.at[f, g], in_sem.at[4 * f + g]
        )
        loads[f, g].start()

    peers = [(right, r), (left, r), (t, other), (right, other), (left, other)]
    barrier = pltpu.get_barrier_semaphore()
    for peer in peers:
        pl.semaphore_signal(barrier, inc=1, device_id=peer, device_id_type=MESH)

    bias_t[...] = jnp.broadcast_to(feat_b[...], (CH, CH)).T
    taps[:, 0] = jnp.zeros((2, 3 * CIN, WIDTH), BF16)

    def split_group(f, g):
        loads[f, g].wait()

        def columns(i, carry):
            part = xin[f, g, pl.ds(16 * i, 16)].reshape(256, 2 * WIDTH)
            found = jnp.dot(part, picks[...], preferred_element_type=F32)
            for b in range(3):
                split[b, pl.ds(256 * i, 256), :] = found[:, b * WIDTH : (b + 1) * WIDTH]
            return carry

        lax.fori_loop(0, 4, columns, 0)

        def regroup(i, carry):
            for b in range(3):
                taps[f, 1 + 16 * g + i, b * CIN : (b + 1) * CIN, :] = split[
                    b, pl.ds(i, CIN, stride=16), :
                ].astype(BF16)
            return carry

        lax.fori_loop(0, 16, regroup, 0, unroll=4)

    def conv_group(f, g):
        def pair(p, carry):
            y = 8 * g + 2 * p
            upper = taps[f, pl.ds(2 * y, 3)].reshape(9 * CIN, WIDTH)
            lower = taps[f, pl.ds(2 * y + 2, 3)].reshape(9 * CIN, WIDTH)
            found = jnp.dot(
                conv_w[...],
                jnp.concatenate([upper, lower], axis=1),
                preferred_element_type=F32,
            )
            for i in range(2):
                feature = found[:, i * WIDTH : (i + 1) * WIDTH] + bias_t[...]
                rows[2 + r, f * BAND + y + i] = jnp.maximum(feature, 0.0).astype(BF16).T
            return carry

        lax.fori_loop(0, 4, pair, 0)

    def remote(src, dst, send, recv, peer):
        return pltpu.make_async_remote_copy(
            src_ref=src, dst_ref=dst, send_sem=send, recv_sem=recv, device_id=peer, device_id_type=MESH
        )

    def row_copy(kind, j):
        window = (2 * (2, 0, 1, 2, 0)[kind]) + r
        place = (1, 1, 1, 2, 0)[kind] * 2 + r
        peer = ((right, r), (left, r), (t, other), (t, other), (t, other))[kind]
        part = pl.ds(GROUP * j, GROUP)
        return remote(
            rows.at[place, part],
            rows.at[window, part],
            row_send.at[kind, j],
            row_recv.at[kind, j],
            peer,
        )

    table_v[2 + r] = sent[0, 0]
    halos = [
        remote(taps.at[f, 64], taps.at[f, 65], halo_send.at[f], halo_recv.at[f], (t, other))
        for f in range(2)
    ]
    tables = []
    for i, peer in enumerate(peers):
        window = (4, 0, 2, 4, 0)[i] + r
        tables.append(remote(table_v.at[2 + r], table_v.at[window], table_send.at[i], table_recv.at[i], peer))

    split_group(0, 3)
    pl.semaphore_wait(barrier, 5)
    for copy in tables:
        copy.start()
    for f in range(2):
        if f:
            split_group(f, 3)
        halos[f].start()
        for g in (3, 2, 1, 0):
            if g:
                split_group(f, g - 1)
            else:
                halos[f].wait()
                above = taps[f, 65]
                taps[f, 0] = jnp.where(r == 0, jnp.zeros_like(above), above)
            conv_group(f, g)
            for kind in range(3):
                row_copy(kind, 4 * f + g).start()

    keep_lane = lax.broadcasted_iota(jnp.int32, (WIDTH, WIDTH), 1)
    keep_x = WIDTH - 1 - lax.broadcasted_iota(jnp.int32, (WIDTH, WIDTH), 0)
    mirror = jnp.where(keep_lane == keep_x, 1.0, 0.0)
    for u in range(SPAN):
        step = keep_lane - lane_of(SPAN * u) % WIDTH
        target = keep_x + step - 8
        valid = (step >= 0) & (step <= 16) & (step % 2 == 0) & (target >= 0) & (target < WIDTH)
        keep[u] = jnp.where(valid, 1.0, 0.0)
    corr_k[...] = lax.dot_general(lanes[...], corr_w[...], NT, preferred_element_type=F32).astype(BF16)
    g1[pl.ds(41 * r, 8)] = jnp.zeros((8, WIDTH, CH), BF16)
    hid[33 * r] = jnp.zeros((WIDTH, 3 * HID), BF16)

    for copy in tables:
        copy.wait()
    to_scalar = pltpu.make_async_copy(table_v, table_s, local_sem)
    to_scalar.start()

    chunk_order = [4 * f + g for f in range(2) for g in (3, 2, 1, 0)]
    for j in chunk_order:
        for kind in range(2):
            row_copy(kind, j).wait_recv()
            row_copy(3 + kind, j).start()
    to_scalar.wait()
    for j in chunk_order:
        for kind in (2, 3, 4):
            row_copy(kind, j).wait_recv()

    def source(j, i):
        slot = slots[0, 0, j, i]
        window = slot // BAND
        row = table_s[window, window // 2, r, slot % BAND]
        weight = jnp.where(row < 2 * BAND, blend[0, 0, j, i], 0.0)
        return weight * rows[window, jnp.minimum(row, 2 * BAND - 1)].astype(F32)

    def ground(y, carry):
        g1[8 + r + y] = (source(BAND + y, 0) + source(BAND + y, 1)).astype(BF16)
        first = (source(y, 0) + source(y, 1)).astype(BF16)
        g0[r + y] = jnp.dot(mirror.astype(BF16), first, preferred_element_type=F32).astype(BF16)
        return carry

    lax.fori_loop(0, BAND, ground, 0)

    edges = [
        remote(
            g1.at[pl.ds(31 - 22 * r, 9)], g1.at[pl.ds(40 * r, 9)], edge_send.at[0], edge_recv.at[0], (t, other)
        ),
        remote(g0.at[31 - 30 * r], g0.at[32 * r], edge_send.at[1], edge_recv.at[1], (t, other)),
    ]
    for copy in edges:
        copy.start()
    for copy in edges:
        copy.wait()

    side = lax.broadcasted_iota(jnp.int32, (WIDTH, HID), 0)

    def hidden(h, carry):
        first = g0[h]
        packed = [jnp.zeros((WIDTH, WIDTH), F32)] * 2
        for u in range(SPAN):
            found = lax.dot_general(first, g1[h + 2 * u], NT, preferred_element_type=F32)
            turned = jnp.concatenate(
                [
                    pltpu.roll(
                        found[k : k + 8], (lane_of(SPAN * u) + 9 + k) % WIDTH, 1, stride=1, stride_axis=0
                    )
                    for k in range(0, WIDTH, 8)
                ],
                axis=0,
            )
            packed[u // 5] = jnp.where(keep[u] > 0.0, turned, packed[u // 5])
        value = jnp.dot((jnp.concatenate(packed, axis=1) * CH**-0.5).astype(BF16), corr_k[...], preferred_element_type=F32)
        value = jnp.maximum(value + corr_b[...], 0.0)
        before = jnp.where(side == 0, 0.0, pltpu.roll(value, 1, 0))
        after = jnp.where(side == WIDTH - 1, 0.0, pltpu.roll(value, WIDTH - 1, 0))
        at = h + 1 - r
        hid[at, :, 0:HID] = after.astype(BF16)
        hid[at, :, HID : 2 * HID] = value.astype(BF16)
        hid[at, :, 2 * HID : 3 * HID] = before.astype(BF16)
        return carry

    lax.fori_loop(0, BAND + 1, hidden, 0, unroll=3)

    def head(i, carry):
        y = 4 * i
        total = None
        for a in range(3):
            part = hid[pl.ds(y + a, 4)].reshape(4 * WIDTH, 3 * HID)
            term = jnp.dot(part, mid_w[a], preferred_element_type=F32)
            total = term if total is None else total + term
        middle = jnp.maximum(total + mid_b[...], 0.0).astype(BF16)
        flow = lax.dot_general(flow_w[...], middle, NT, preferred_element_type=F32)
        for c in range(2):
            for k in range(4):
                out[0, c, pl.ds(y + k, 1), :] = flow[c : c + 1, k * WIDTH : (k + 1) * WIDTH] + flow_b[c]
        return carry

    lax.fori_loop(0, BAND // 4, head, 0)
    for c in range(2):
        out[0, c] = jnp.dot(
            out[0, c], mirror, preferred_element_type=F32, precision=lax.Precision.HIGHEST
        )

    for j in chunk_order:
        for kind in range(5):
            row_copy(kind, j).wait_send()


def on_device(
    tiles,
    frames,
    feat_weight,
    feat_bias,
    send_rows,
    recv_slots,
    blend,
    corr_weight,
    corr_bias,
    mid_weight,
    mid_bias,
    flow_weight,
    flow_bias,
):
    conv_w = feat_weight.transpose(1, 0, 2).reshape(CH, 9 * CIN)
    mid_w = mid_weight.transpose(0, 2, 1).reshape(3, 3 * HID, MID)
    vmem = pl.BlockSpec(memory_space=pltpu.VMEM)
    smem = pl.BlockSpec(memory_space=pltpu.SMEM)
    dma = pltpu.SemaphoreType.DMA
    return pl.pallas_call(
        functools.partial(kernel, tiles),
        out_shape=jax.ShapeDtypeStruct((1, 2, BAND, WIDTH), F32),
        in_specs=[pl.BlockSpec(memory_space=pl.ANY)]
        + [vmem] * 4
        + [smem] * 2
        + [vmem] * 6
        + [smem],
        out_specs=vmem,
        scratch_shapes=[
            pltpu.VMEM((2, 4, CIN, 16, 2 * WIDTH), BF16),
            pltpu.VMEM((3, 16 * CIN, WIDTH), F32),
            pltpu.VMEM((2, 66, 3 * CIN, WIDTH), BF16),
            pltpu.VMEM((CH, CH), F32),
            pltpu.VMEM((6, 2 * BAND, WIDTH, CH), BF16),
            pltpu.VMEM((6, 3, 2, BAND), jnp.int32),
            pltpu.SMEM((6, 3, 2, BAND), jnp.int32),
            pltpu.VMEM((BAND + 1, WIDTH, CH), BF16),
            pltpu.VMEM((BAND + 17, WIDTH, CH), BF16),
            pltpu.VMEM((SPAN, WIDTH, WIDTH), F32),
            pltpu.VMEM((2 * WIDTH, HID), BF16),
            pltpu.VMEM((BAND + 2, WIDTH, 3 * HID), BF16),
            dma((8,)),
            dma((2,)),
            dma((2,)),
            dma((5, CHUNKS)),
            dma((5, CHUNKS)),
            dma((5,)),
            dma((5,)),
            dma((2,)),
            dma((2,)),
            dma,
        ],
        compiler_params=pltpu.CompilerParams(
            collective_id=0, has_side_effects=True, vmem_limit_bytes=56 * 1024 * 1024
        ),
    )(
        frames,
        jnp.asarray(column_picks(), BF16),
        conv_w,
        feat_bias.reshape(1, CH),
        send_rows,
        recv_slots,
        blend,
        jnp.asarray(offset_lanes(), BF16),
        corr_weight,
        corr_bias.reshape(1, HID),
        mid_w,
        mid_bias.reshape(1, MID),
        flow_weight,
        flow_bias,
    )


def solution(mesh):
    return jax.shard_map(
        functools.partial(on_device, mesh.shape["tiles"]),
        mesh=mesh,
        in_specs=(
            P("tiles", None, None, "rows", None),
            P(),
            P(),
            P("tiles", "rows", None, None, None),
            P("tiles", "rows", None, None),
            P("tiles", "rows", None, None),
            P(),
            P(),
            P(),
            P(),
            P(),
            P(),
        ),
        out_specs=P("tiles", None, "rows", None),
        check_vma=False,
    )
```

profile of v0, /device:TPU:1, one launch (start us, length us, event | category | flops | bytes accessed | tf_op | source)
XLA Modules:
  0.0 104.4 jit_solution(9606301409053315921)
XLA Ops:
  0.0 1.4 %copy.22.slots = s32[1,1,64,2]{3,2,1,0:T(8,128)} copy(s32[1,1,64,2]{2,3,1,0:T(2,128)} %param.18) | data formatting | bytes 1024 | tf_op args[4]
  1.4 1.4 %copy.23.blend = f32[1,1,64,2]{3,2,1,0:T(8,128)} copy(f32[1,1,64,2]{2,3,1,0:T(2,128)} %param.19) | data formatting | bytes 1024 | tf_op args[5]
  2.8 1.5 %copy.24.corr_w = bf16[256,81]{1,0:T(8,128)(2,1)} copy(bf16[256,81]{0,1:T(8,128)(2,1)} %param.20) | data formatting | bytes 82944 | tf_op args[6]
  4.3 1.7 %copy.21.conv_w = bf16[128,576]{1,0:T(8,128)(2,1)} copy(bf16[128,576]{0,1:T(8,128)(2,1)} %bitcast.10) | data formatting | bytes 294912 | tf_op jit(solution)/shard_map/reshape | solution.py:317
  6.0 2.3 %copy.20 = bf16[9,256,192]{2,1,0:T(8,128)(2,1)} copy(bf16[9,256,192]{1,2,0:T(8,128)(2,1)} %bitcast.9) | data formatting | bytes 1769472 | tf_op jit(solution)/shard_map/transpose | solution.py:318
  8.3 94.7 %shard_map.136 = f32[1,2,32,128]{3,2,1,0:T(8,128)} custom-call(bf16[1,2,64,64,256]{4,3,2,1,0:T(8,128)(2,1)} %frames.1, bf16[256,384]{1,0:T(8,128)(2,1)} %constant.4.clone.picks, bf16[128,576]{1,0:T(8,128)(2,1)} %copy.21.conv_w, f32[1,128]{1,0:T(1,128)} %bitcast.13, s32[1,1,3,2,32]{4,3,2,1,0:T(2,128)} %sent.1, s32[1,1,64,2]{3,2,1,0:T(8,128)} %copy.22.slots, ...), custom_call_target="tpu_custom_call" | custom-call | tf_op jit(solution)/shard_map/pallas_call | solution.py:322
  103.0 1.4 %copy.26 = f32[1,2,32,128]{3,2,1,0:T(8,128)} copy(f32[1,2,32,128]{3,2,1,0:T(8,128)} %shard_map.136) | data formatting | bytes 65536
where the time goes:
time: 105 us; the launch traced here: 104 us
  Pallas kernels  94.7 us (90%)
  local copies, waits for them, and re-layouts  9.7 us (9%)
    pallas_call x1, Pallas kernels, on_device(): pl.pallas_call(functools.partial(kernel, tiles), out_shape=jax.ShapeDtype...  94.7 us
    unnamed x4, local copies, waits for them, and re-layouts  5.64 us
    transpose x1, local copies, waits for them, and re-layouts, on_device(): mid_w = mid_weight.transpose(0, 2, 1).reshape(3, 3 * HID, MID)  2.34 us

commit v1 on v0

v1 whole, which is shorter than its diff:
```python
import functools

import jax
import jax.numpy as jnp
import numpy as np
from jax import lax
from jax.experimental import pallas as pl
from jax.experimental.pallas import tpu as pltpu
from jax.sharding import PartitionSpec as P

BF16 = jnp.bfloat16
F32 = jnp.float32
MESH = pl.DeviceIdType.MESH

CIN = 64
CH = 128
HID = 256
MID = 192
WIDTH = 128
BAND = 32
GROUP = 8
GROUPS = 2 * BAND // GROUP
SPAN = 9
NT = (((1,), (1,)), ((), ()))
TN = (((0,), (0,)), ((), ()))

PARTS = (((0, 96), (0, 80), (0, 64)), ((96, 128), (80, 128), (64, 128)))


def centre_of(step_row):
    return 24 * (step_row % 5) + 15


def offset_lanes():
    lanes = np.zeros((2 * WIDTH, SPAN * SPAN), np.float32)
    for offset in range(SPAN * SPAN):
        step_row, step_col = offset // SPAN, offset % SPAN
        lanes[WIDTH * (step_row // 5) + centre_of(step_row) + 8 - 2 * step_col, offset] = 1.0
    return lanes


def kernel(
    tiles,
    frames,
    feat_w,
    feat_b,
    sent,
    slots,
    blend,
    lanes,
    corr_w,
    corr_b,
    mid_w,
    mid_b,
    flow_w,
    flow_b,
    out,
    xin,
    picks,
    conv_w,
    split,
    taps,
    bias_t,
    rows_0,
    rows_1,
    table_v,
    table_s,
    g0,
    g1,
    g1_t,
    halo,
    mirror,
    packed,
    corr_k,
    tail,
    hid,
    mid_in,
    mid_k,
    in_sem,
    halo_send,
    halo_recv,
    row_send,
    row_recv,
    table_send,
    table_recv,
    edge_send,
    edge_recv,
    local_sem,
):
    t = lax.axis_index("tiles")
    r = lax.axis_index("rows")
    right, left = lax.rem(t + 1, tiles), lax.rem(t + tiles - 1, tiles)
    other = 1 - r
    rows = (rows_0, rows_1)

    order = [(f, g) for f in range(2) for g in (3, 2, 1, 0)]
    loads = {}
    for f, g in order:
        loads[f, g] = pltpu.make_async_copy(
            frames.at[0, f, :, pl.ds(16 * g, 16), :], xin.at[f, g], in_sem.at[4 * f + g]
        )
        loads[f, g].start()
    mid_load = pltpu.make_async_copy(mid_w, mid_in, local_sem.at[0])
    mid_load.start()

    peers = [(right, r), (left, r), (t, other), (right, other), (left, other)]
    barrier = pltpu.get_barrier_semaphore()
    for peer in peers:
        pl.semaphore_signal(barrier, inc=1, device_id=peer, device_id_type=MESH)

    column = lax.broadcasted_iota(jnp.int32, (2 * WIDTH, WIDTH), 0)
    target = lax.broadcasted_iota(jnp.int32, (2 * WIDTH, WIDTH), 1)
    for b in range(3):
        picks[:, b * WIDTH : (b + 1) * WIDTH] = jnp.where(column == 2 * target - 1 + b, 1.0, 0.0).astype(BF16)
    conv_w[...] = feat_w[...].T
    bias_t[...] = jnp.broadcast_to(feat_b[...], (CH, CH)).T
    taps[:, 0] = jnp.zeros((2, 3 * CIN, WIDTH), BF16)

    def split_group(f, g):
        loads[f, g].wait()

        def columns(i, carry):
            part = xin[f, g, pl.ds(16 * i, 16)].reshape(256, 2 * WIDTH)
            found = jnp.dot(part, picks[...], preferred_element_type=F32)
            for b in range(3):
                split[b, pl.ds(256 * i, 256), :] = found[:, b * WIDTH : (b + 1) * WIDTH]
            return carry

        lax.fori_loop(0, 4, columns, 0)

        def regroup(i, carry):
            for b in range(3):
                taps[f, 1 + 16 * g + i, b * CIN : (b + 1) * CIN, :] = split[
                    b, pl.ds(i, CIN, stride=16), :
                ].astype(BF16)
            return carry

        lax.fori_loop(0, 16, regroup, 0, unroll=4)

    def conv_group(f, g):
        def pair(p, carry):
            y = 8 * g + 2 * p
            upper = taps[f, pl.ds(2 * y, 3)].reshape(9 * CIN, WIDTH)
            lower = taps[f, pl.ds(2 * y + 2, 3)].reshape(9 * CIN, WIDTH)
            found = jnp.dot(
                conv_w[...],
                jnp.concatenate([upper, lower], axis=1),
                preferred_element_type=F32,
            )
            for i in range(2):
                feature = found[:, i * WIDTH : (i + 1) * WIDTH] + bias_t[...]
                feature = jnp.maximum(feature, 0.0).astype(BF16).T
                for k in range(len(PARTS)):
                    low, high = PARTS[k][0]
                    rows[k][2 + r, f * BAND + y + i] = feature[low:high]
            return carry

        lax.fori_loop(0, 4, pair, 0)

    def remote(src, dst, send, recv, peer):
        return pltpu.make_async_remote_copy(
            src_ref=src, dst_ref=dst, send_sem=send, recv_sem=recv, device_id=peer, device_id_type=MESH
        )

    def row_copy(kind, k, j):
        window = 2 * (2, 0, 1, 2, 0)[kind] + r
        place = 2 * (1, 1, 1, 2, 0)[kind] + r
        peer = ((right, r), (left, r), (t, other), (t, other), (t, other))[kind]
        part = pl.ds(GROUP * j, GROUP)
        return remote(
            rows[k].at[place, part],
            rows[k].at[window, part],
            row_send.at[kind, k, j],
            row_recv.at[kind, k, j],
            peer,
        )

    table_v[2 + r] = sent[0, 0]
    halos = [
        remote(taps.at[f, 64], taps.at[f, 65], halo_send.at[f], halo_recv.at[f], (t, other))
        for f in range(2)
    ]
    tables = []
    for i, peer in enumerate(peers):
        window = (4, 0, 2, 4, 0)[i] + r
        tables.append(remote(table_v.at[2 + r], table_v.at[window], table_send.at[i], table_recv.at[i], peer))

    split_group(0, 3)
    pl.semaphore_wait(barrier, 5)
    for f in range(2):
        if f:
            split_group(f, 3)
        halos[f].start()
        for g in (3, 2, 1, 0):
            if g:
                split_group(f, g - 1)
            else:
                halos[f].wait()
                above = taps[f, 65]
                taps[f, 0] = jnp.where(r == 0, jnp.zeros_like(above), above)
            conv_group(f, g)
            for kind in range(3):
                row_copy(kind, 0, 4 * f + g).start()
        if f == 0:
            for copy in tables:
                copy.start()
    group_order = [4 * f + g for f, g in order]
    for k in range(1, len(PARTS)):
        for j in group_order:
            for kind in range(3):
                row_copy(kind, k, j).start()

    lane = lax.broadcasted_iota(jnp.int32, (WIDTH, WIDTH), 1)
    place = lax.broadcasted_iota(jnp.int32, (WIDTH, WIDTH), 0)
    mirror[...] = jnp.where(lane == WIDTH - 1 - place, 1.0, 0.0).astype(BF16)
    corr_k[...] = jnp.dot(lanes[...], corr_w[...], preferred_element_type=F32).astype(BF16)
    hid[33 * r] = jnp.zeros((WIDTH, 3 * HID), BF16)

    def clear(i, carry):
        packed[i] = jnp.zeros((WIDTH, 2 * WIDTH), F32)
        return carry

    lax.fori_loop(0, BAND, clear, 0)

    def clear_rim(i, carry):
        g1_t[i % 2 * 24 + 20 * r + i // 2] = jnp.zeros((CH, WIDTH), BF16)
        return carry

    lax.fori_loop(0, 8, clear_rim, 0)
    mid_load.wait()
    for tap in range(9):
        a, b = tap // 3, tap % 3
        mid_k[a, b * HID : (b + 1) * HID, :] = mid_in[tap].T

    for copy in tables:
        copy.wait()
    to_scalar = pltpu.make_async_copy(table_v, table_s, local_sem.at[1])
    to_scalar.start()
    to_scalar.wait()

    lane8 = lax.broadcasted_iota(jnp.int32, (8, WIDTH), 1)
    place8 = lax.broadcasted_iota(jnp.int32, (8, WIDTH), 0)

    def do_part(k):
        (a0, a1), (c0, c1), (m0, m1) = PARTS[k]
        width = c1 - c0

        for j in group_order:
            for kind in range(2):
                row_copy(kind, k, j).wait_recv()
                row_copy(3 + kind, k, j).start()
        for j in group_order:
            for kind in (2, 3, 4):
                row_copy(kind, k, j).wait_recv()

        def source(j, i):
            slot = slots[0, 0, i, j]
            window = slot // BAND
            row = table_s[window, window // 2, r, slot % BAND]
            weight = jnp.where(row < 2 * BAND, blend[0, 0, i, j], 0.0)
            return weight * rows[k][window, jnp.minimum(row, 2 * BAND - 1)].astype(F32)

        def turn(where, value):
            turned = lax.dot_general(value, mirror[a0:a1], TN, preferred_element_type=F32).astype(BF16)
            if k:
                turned = g1_t[where] + turned
            g1_t[where] = turned

        def ground(i, carry):
            y = lax.rem(24 * other + i, BAND)
            parity, half = lax.rem(y, 2), y // 2
            g0[16 * parity + half, a0:a1] = (source(y, 0) + source(y, 1)).astype(BF16)
            second = (source(BAND + y, 0) + source(BAND + y, 1)).astype(BF16)
            g1[y, a0:a1] = second
            turn(24 * parity + 4 + half, second)
            return carry

        lax.fori_loop(0, 8, ground, 0, unroll=2)
        edge = remote(
            g1.at[pl.ds(24 * other, 8), pl.ds(a0, a1 - a0)],
            halo.at[:, pl.ds(a0, a1 - a0)],
            edge_send.at[0, k],
            edge_recv.at[0, k],
            (t, other),
        )
        edge.start()
        lax.fori_loop(8, BAND, ground, 0, unroll=2)
        edge.wait()

        def ground_halo(i, carry):
            turn(24 * lax.rem(i, 2) + 20 * other + i // 2, halo[i, a0:a1])
            return carry

        lax.fori_loop(0, 8, ground_halo, 0, unroll=2)

        def correlate(b, carry):
            parity, block = lax.rem(b, 2), b // 2
            first = 16 * parity + 4 * block
            second = 24 * parity + 4 * block
            for j in range(0, 12, 2):
                low, high = max(0, j - 8), min(4, j + 2)
                left_side = g0[pl.ds(first + low, high - low), c0:c1].reshape((high - low) * width, CH)
                pair = jnp.concatenate([g1_t[second + j], g1_t[second + j + 1]], axis=1)
                found = jnp.dot(left_side, pair, preferred_element_type=F32)
                for h in range(low, high):
                    for e in range(2):
                        u = j + e - h
                        if not 0 <= u < SPAN:
                            continue
                        centre = centre_of(u)
                        for x in range(c0, c1, 8):
                            at = (h - low) * width + x - c0
                            turned = pltpu.roll(
                                found[at : at + 8, e * WIDTH : (e + 1) * WIDTH],
                                (centre + 1 + x) % WIDTH,
                                1,
                                stride=1,
                                stride_axis=0,
                            )
                            mask = (lane8 >= centre - 8) & (lane8 <= centre + 8)
                            if x == 0:
                                mask = mask & (place8 + centre - lane8 >= 0)
                            if x == WIDTH - 8:
                                mask = mask & (place8 + centre - lane8 < 8)
                            pltpu.store(
                                packed.at[
                                    first + h, pl.ds(x, 8), pl.ds(WIDTH * (u // 5), WIDTH)
                                ],
                                turned,
                                mask=mask,
                            )
            return carry

        lax.fori_loop(0, 8, correlate, 0)

        kept = 16 if k else 0
        side = lax.broadcasted_iota(jnp.int32, (width + kept, HID), 0)

        def hidden(i, carry):
            at = 2 * lax.rem(i, 16) + i // 16 + 1
            scaled = (packed[i, c0:c1] * CH**-0.5).astype(BF16)
            value = jnp.dot(scaled, corr_k[...], preferred_element_type=F32)
            value = jnp.maximum(value + corr_b[...], 0.0)
            whole = jnp.concatenate([tail[i], value], axis=0) if k else value
            before = pltpu.roll(whole, 1, 0)
            after = pltpu.roll(whole, width + kept - 1, 0)
            if k == 0:
                before = jnp.where(side == 0, 0.0, before)
            if k == len(PARTS) - 1:
                after = jnp.where(side == width + kept - 1, 0.0, after)
            else:
                tail[i] = value[width - 16 :]
            hid[at, c0:c1, 0:HID] = before[kept:].astype(BF16)
            hid[at, c0:c1, HID : 2 * HID] = value.astype(BF16)
            hid[at, m0:m1, 2 * HID : 3 * HID] = after[0 : m1 - m0].astype(BF16)
            return carry

        lax.fori_loop(0, BAND, hidden, 0, unroll=4)

        rim = remote(
            hid.at[32 - 31 * r, pl.ds(m0, m1 - m0)],
            hid.at[33 * r, pl.ds(m0, m1 - m0)],
            edge_send.at[1, k],
            edge_recv.at[1, k],
            (t, other),
        )
        rim_in = remote(
            hid.at[32 - 31 * r, pl.ds(m0, m1 - m0)],
            hid.at[33 * other, pl.ds(m0, m1 - m0)],
            edge_send.at[1, k],
            edge_recv.at[1, k],
            (t, other),
        )
        rim.start()
        columns = m1 - m0

        def head(i, carry):
            y = 8 * lax.rem(i + r, 4)
            total = None
            for a in range(3):
                part = hid[pl.ds(y + a, 8), m0:m1].reshape(8 * columns, 3 * HID)
                term = jnp.dot(part, mid_k[a], preferred_element_type=F32)
                total = term if total is None else total + term
            middle = jnp.maximum(total + mid_b[...], 0.0).astype(BF16)
            flow = lax.dot_general(flow_w[...], middle, NT, preferred_element_type=F32)
            for c in range(2):
                for n in range(8):
                    out[0, c, pl.ds(y + n, 1), m0:m1] = (
                        flow[c : c + 1, n * columns : (n + 1) * columns] + flow_b[c]
                    )
            return carry

        lax.fori_loop(0, 3, head, 0)
        rim.wait_send()
        rim_in.wait_recv()
        head(3, 0)

    for k in range(len(PARTS)):
        do_part(k)

    for k in range(len(PARTS)):
        for j in group_order:
            for kind in range(5):
                row_copy(kind, k, j).wait_send()


def on_device(
    tiles,
    frames,
    feat_weight,
    feat_bias,
    send_rows,
    recv_slots,
    blend,
    corr_weight,
    corr_bias,
    mid_weight,
    mid_bias,
    flow_weight,
    flow_bias,
):
    vmem = pl.BlockSpec(memory_space=pltpu.VMEM)
    smem = pl.BlockSpec(memory_space=pltpu.SMEM)
    hbm = pl.BlockSpec(memory_space=pl.ANY)
    dma = pltpu.SemaphoreType.DMA
    parts = len(PARTS)
    return pl.pallas_call(
        functools.partial(kernel, tiles),
        out_shape=jax.ShapeDtypeStruct((1, 2, BAND, WIDTH), F32),
        in_specs=[hbm, vmem, vmem, vmem, smem, smem, vmem, vmem, vmem, hbm, vmem, vmem, smem],
        out_specs=vmem,
        scratch_shapes=[
            pltpu.VMEM((2, 4, CIN, 16, 2 * WIDTH), BF16),
            pltpu.VMEM((2 * WIDTH, 3 * WIDTH), BF16),
            pltpu.VMEM((CH, 9 * CIN), BF16),
            pltpu.VMEM((3, 16 * CIN, WIDTH), F32),
            pltpu.VMEM((2, 66, 3 * CIN, WIDTH), BF16),
            pltpu.VMEM((CH, CH), F32),
            pltpu.VMEM((6, 2 * BAND, PARTS[0][0][1] - PARTS[0][0][0], CH), BF16),
            pltpu.VMEM((6, 2 * BAND, PARTS[1][0][1] - PARTS[1][0][0], CH), BF16),
            pltpu.VMEM((6, 3, 2, BAND), jnp.int32),
            pltpu.SMEM((6, 3, 2, BAND), jnp.int32),
            pltpu.VMEM((BAND, WIDTH, CH), BF16),
            pltpu.VMEM((BAND, WIDTH, CH), BF16),
            pltpu.VMEM((BAND + 16, CH, WIDTH), BF16),
            pltpu.VMEM((8, WIDTH, CH), BF16),
            pltpu.VMEM((WIDTH, WIDTH), BF16),
            pltpu.VMEM((BAND, WIDTH, 2 * WIDTH), F32),
            pltpu.VMEM((2 * WIDTH, HID), BF16),
            pltpu.VMEM((BAND, 16, HID), F32),
            pltpu.VMEM((BAND + 2, WIDTH, 3 * HID), BF16),
            pltpu.VMEM((9, MID, HID), BF16),
            pltpu.VMEM((3, 3 * HID, MID), BF16),
            dma((8,)),
            dma((2,)),
            dma((2,)),
            dma((5, parts, GROUPS)),
            dma((5, parts, GROUPS)),
            dma((5,)),
            dma((5,)),
            dma((2, parts)),
            dma((2, parts)),
            dma((2,)),
        ],
        compiler_params=pltpu.CompilerParams(
            collective_id=0, has_side_effects=True, vmem_limit_bytes=60 * 1024 * 1024
        ),
    )(
        frames,
        feat_weight.transpose(0, 2, 1).reshape(9 * CIN, CH),
        feat_bias.reshape(1, CH),
        send_rows,
        recv_slots.transpose(0, 1, 3, 2),
        blend.transpose(0, 1, 3, 2),
        jnp.asarray(offset_lanes(), BF16),
        corr_weight.T,
        corr_bias.reshape(1, HID),
        mid_weight,
        mid_bias.reshape(1, MID),
        flow_weight,
        flow_bias,
    )


def solution(mesh):
    return jax.shard_map(
        functools.partial(on_device, mesh.shape["tiles"]),
        mesh=mesh,
        in_specs=(
            P("tiles", None, None, "rows", None),
            P(),
            P(),
            P("tiles", "rows", None, None, None),
            P("tiles", "rows", None, None),
            P("tiles", "rows", None, None),
            P(),
            P(),
            P(),
            P(),
            P(),
            P(),
        ),
        out_specs=P("tiles", None, "rows", None),
        check_vma=False,
    )
```

time: 105 us -> 90.2 us (0.86)
  local copies, waits for them, and re-layouts: 9.7 us -> 1.38 us
  Pallas kernels: 94.7 us -> 88.4 us
    pallas_call x1, Pallas kernels: 94.7 us -> 88.4 us  [on_device(): pl.pallas_call(functools.partial(kernel, tiles), out_shape=jax.ShapeDtype...]
    unnamed x4 -> x1, local copies, waits for them, and re-layouts: 5.64 us -> 1.38 us
    transpose x1 -> x0, local copies, waits for them, and re-layouts: 2.34 us -> none  [on_device(): mid_w = mid_weight.transpose(0, 2, 1).reshape(3, 3 * HID, MID)]
    reshape x1 -> x0, local copies, waits for them, and re-layouts: 1.72 us -> none  [on_device(): conv_w = feat_weight.transpose(1, 0, 2).reshape(CH, 9 * CIN)]
where the time goes in v1:
time: 90.2 us; the launch traced here: 89.8 us
  Pallas kernels  88.4 us (98%)
  local copies, waits for them, and re-layouts  1.38 us (2%)
    pallas_call x1, Pallas kernels, on_device(): pl.pallas_call(functools.partial(kernel, tiles), out_shape=jax.ShapeDtype...  88.4 us

profile of v1, /device:TPU:1, one launch (start us, length us, event | category | flops | bytes accessed | tf_op | source)
XLA Modules:
  0.0 89.8 jit_solution(3785714186009807659)
XLA Ops:
  0.0 88.4 %shard_map.127 = f32[1,2,32,128]{3,2,1,0:T(8,128)} custom-call(bf16[1,2,64,64,256]{4,3,2,1,0:T(8,128)(2,1)} %frames.1, bf16[576,128]{1,0:T(8,128)(2,1)} %bitcast.9, f32[1,128]{1,0:T(1,128)} %bitcast.15, s32[1,1,3,2,32]{4,3,2,1,0:T(2,128)} %sent.1, s32[1,1,2,64]{3,2,1,0:T(2,128)} %bitcast.11, f32[1,1,2,64]{3,2,1,0:T(2,128)} %bitcast.12, ...), custom_call_target="tpu_custom_call" | custom-call | tf_op jit(solution)/shard_map/pallas_call | solution.py:427
  88.4 1.4 %copy.15 = f32[1,2,32,128]{3,2,1,0:T(8,128)} copy(f32[1,2,32,128]{3,2,1,0:T(8,128)} %shard_map.127) | data formatting | bytes 65536

commit v2 on v1

--- a/solution.py
+++ b/solution.py
@@ -24,7 +24,11 @@
 NT = (((1,), (1,)), ((), ()))
 TN = (((0,), (0,)), ((), ()))
 
-PARTS = (((0, 96), (0, 80), (0, 64)), ((96, 128), (80, 128), (64, 128)))
+PARTS = (
+    ((0, 80), (0, 64), (0, 48)),
+    ((80, 128), (64, 128), (48, 128)),
+
+)
 
 
 def centre_of(step_row):
@@ -61,10 +65,40 @@
     split,
     taps,
     bias_t,
-    rows_0,
-    rows_1,
+    *rest,
+):
+    rows, rest = rest[: len(PARTS)], rest[len(PARTS) :]
+    run(tiles, frames, feat_w, feat_b, sent, slots, blend, lanes, corr_w, corr_b, mid_w, mid_b,
+        flow_w, flow_b, out, xin, picks, conv_w, split, taps, bias_t, rows, *rest)
+
+
+def run(
+    tiles,
+    frames,
+    feat_w,
+    feat_b,
+    sent,
+    slots,
+    blend,
+    lanes,
+    corr_w,
+    corr_b,
+    mid_w,
+    mid_b,
+    flow_w,
+    flow_b,
+    out,
+    xin,
+    picks,
+    conv_w,
+    split,
+    taps,
+    bias_t,
+    rows,
     table_v,
     table_s,
+    row_of,
+    weight_of,
     g0,
     g1,
     g1_t,
@@ -91,7 +125,6 @@
     r = lax.axis_index("rows")
     right, left = lax.rem(t + 1, tiles), lax.rem(t + tiles - 1, tiles)
     other = 1 - r
-    rows = (rows_0, rows_1)
 
     order = [(f, g) for f in range(2) for g in (3, 2, 1, 0)]
     loads = {}
@@ -126,7 +159,7 @@
                 split[b, pl.ds(256 * i, 256), :] = found[:, b * WIDTH : (b + 1) * WIDTH]
             return carry
 
-        lax.fori_loop(0, 4, columns, 0)
+        lax.fori_loop(0, 4, columns, 0, unroll=2)
 
         def regroup(i, carry):
             for b in range(3):
@@ -135,7 +168,7 @@
                 ].astype(BF16)
             return carry
 
-        lax.fori_loop(0, 16, regroup, 0, unroll=4)
+        lax.fori_loop(0, 16, regroup, 0, unroll=8)
 
     def conv_group(f, g):
         def pair(p, carry):
@@ -152,10 +185,10 @@
                 feature = jnp.maximum(feature, 0.0).astype(BF16).T
                 for k in range(len(PARTS)):
                     low, high = PARTS[k][0]
-                    rows[k][2 + r, f * BAND + y + i] = feature[low:high]
-            return carry
-
-        lax.fori_loop(0, 4, pair, 0)
+                    rows[k][2 * BAND * (2 + r) + f * BAND + y + i] = feature[low:high]
+            return carry
+
+        lax.fori_loop(0, 4, pair, 0, unroll=2)
 
     def remote(src, dst, send, recv, peer):
         return pltpu.make_async_remote_copy(
@@ -166,10 +199,9 @@
         window = 2 * (2, 0, 1, 2, 0)[kind] + r
         place = 2 * (1, 1, 1, 2, 0)[kind] + r
         peer = ((right, r), (left, r), (t, other), (t, other), (t, other))[kind]
-        part = pl.ds(GROUP * j, GROUP)
         return remote(
-            rows[k].at[place, part],
-            rows[k].at[window, part],
+            rows[k].at[pl.ds(2 * BAND * place + GROUP * j, GROUP)],
+            rows[k].at[pl.ds(2 * BAND * window + GROUP * j, GROUP)],
             row_send.at[kind, k, j],
             row_recv.at[kind, k, j],
             peer,
@@ -238,27 +270,37 @@
     to_scalar.start()
     to_scalar.wait()
 
+    def look_up(j, carry):
+        for i in range(2):
+            slot = slots[0, 0, i, j]
+            window = slot // BAND
+            row = table_s[window, window // 2, r, slot % BAND]
+            row_of[i, j] = 2 * BAND * window + jnp.minimum(row, 2 * BAND - 1)
+            weight_of[i, j] = jnp.where(row < 2 * BAND, blend[0, 0, i, j], 0.0)
+        return carry
+
+    lax.fori_loop(0, 2 * BAND, look_up, 0, unroll=4)
+
     lane8 = lax.broadcasted_iota(jnp.int32, (8, WIDTH), 1)
     place8 = lax.broadcasted_iota(jnp.int32, (8, WIDTH), 0)
 
-    def do_part(k):
-        (a0, a1), (c0, c1), (m0, m1) = PARTS[k]
-        width = c1 - c0
-
+    def forward(k):
         for j in group_order:
             for kind in range(2):
                 row_copy(kind, k, j).wait_recv()
                 row_copy(3 + kind, k, j).start()
+
+    def do_part(k):
+        (a0, a1), (c0, c1), (m0, m1) = PARTS[k]
+        width = c1 - c0
+
+        forward(k)
         for j in group_order:
             for kind in (2, 3, 4):
                 row_copy(kind, k, j).wait_recv()
 
         def source(j, i):
-            slot = slots[0, 0, i, j]
-            window = slot // BAND
-            row = table_s[window, window // 2, r, slot % BAND]
-            weight = jnp.where(row < 2 * BAND, blend[0, 0, i, j], 0.0)
-            return weight * rows[k][window, jnp.minimum(row, 2 * BAND - 1)].astype(F32)
+            return weight_of[i, j] * rows[k][row_of[i, j]].astype(F32)
 
         def turn(where, value):
             turned = lax.dot_general(value, mirror[a0:a1], TN, preferred_element_type=F32).astype(BF16)
@@ -275,7 +317,7 @@
             turn(24 * parity + 4 + half, second)
             return carry
 
-        lax.fori_loop(0, 8, ground, 0, unroll=2)
+        lax.fori_loop(0, 8, ground, 0, unroll=4)
         edge = remote(
             g1.at[pl.ds(24 * other, 8), pl.ds(a0, a1 - a0)],
             halo.at[:, pl.ds(a0, a1 - a0)],
@@ -284,14 +326,14 @@
             (t, other),
         )
         edge.start()
-        lax.fori_loop(8, BAND, ground, 0, unroll=2)
+        lax.fori_loop(8, BAND, ground, 0, unroll=4)
         edge.wait()
 
         def ground_halo(i, carry):
             turn(24 * lax.rem(i, 2) + 20 * other + i // 2, halo[i, a0:a1])
             return carry
 
-        lax.fori_loop(0, 8, ground_halo, 0, unroll=2)
+        lax.fori_loop(0, 8, ground_halo, 0, unroll=8)
 
         def correlate(b, carry):
             parity, block = lax.rem(b, 2), b // 2
@@ -331,31 +373,34 @@
                             )
             return carry
 
-        lax.fori_loop(0, 8, correlate, 0)
+        lax.fori_loop(0, 8, correlate, 0, unroll=2)
 
         kept = 16 if k else 0
         side = lax.broadcasted_iota(jnp.int32, (width + kept, HID), 0)
 
-        def hidden(i, carry):
-            at = 2 * lax.rem(i, 16) + i // 16 + 1
-            scaled = (packed[i, c0:c1] * CH**-0.5).astype(BF16)
-            value = jnp.dot(scaled, corr_k[...], preferred_element_type=F32)
-            value = jnp.maximum(value + corr_b[...], 0.0)
-            whole = jnp.concatenate([tail[i], value], axis=0) if k else value
-            before = pltpu.roll(whole, 1, 0)
-            after = pltpu.roll(whole, width + kept - 1, 0)
-            if k == 0:
-                before = jnp.where(side == 0, 0.0, before)
-            if k == len(PARTS) - 1:
-                after = jnp.where(side == width + kept - 1, 0.0, after)
-            else:
-                tail[i] = value[width - 16 :]
-            hid[at, c0:c1, 0:HID] = before[kept:].astype(BF16)
-            hid[at, c0:c1, HID : 2 * HID] = value.astype(BF16)
-            hid[at, m0:m1, 2 * HID : 3 * HID] = after[0 : m1 - m0].astype(BF16)
-            return carry
-
-        lax.fori_loop(0, BAND, hidden, 0, unroll=4)
+        def hidden(q, carry):
+            scaled = (packed[pl.ds(4 * q, 4), c0:c1] * CH**-0.5).astype(BF16).reshape(4 * width, 2 * WIDTH)
+            found = jnp.dot(scaled, corr_k[...], preferred_element_type=F32)
+            found = jnp.maximum(found + corr_b[...], 0.0)
+            for n in range(4):
+                i = 4 * q + n
+                at = 2 * lax.rem(i, 16) + i // 16 + 1
+                value = found[n * width : (n + 1) * width]
+                whole = jnp.concatenate([tail[i], value], axis=0) if k else value
+                before = pltpu.roll(whole, 1, 0)
+                after = pltpu.roll(whole, width + kept - 1, 0)
+                if k == 0:
+                    before = jnp.where(side == 0, 0.0, before)
+                if k == len(PARTS) - 1:
+                    after = jnp.where(side == width + kept - 1, 0.0, after)
+                else:
+                    tail[i] = value[width - 16 :]
+                hid[at, c0:c1, 0:HID] = before[kept:].astype(BF16)
+                hid[at, c0:c1, HID : 2 * HID] = value.astype(BF16)
+                hid[at, m0:m1, 2 * HID : 3 * HID] = after[0 : m1 - m0].astype(BF16)
+            return carry
+
+        lax.fori_loop(0, BAND // 4, hidden, 0, unroll=2)
 
         rim = remote(
             hid.at[32 - 31 * r, pl.ds(m0, m1 - m0)],
@@ -436,10 +481,11 @@
             pltpu.VMEM((3, 16 * CIN, WIDTH), F32),
             pltpu.VMEM((2, 66, 3 * CIN, WIDTH), BF16),
             pltpu.VMEM((CH, CH), F32),
-            pltpu.VMEM((6, 2 * BAND, PARTS[0][0][1] - PARTS[0][0][0], CH), BF16),
-            pltpu.VMEM((6, 2 * BAND, PARTS[1][0][1] - PARTS[1][0][0], CH), BF16),
+            *[pltpu.VMEM((12 * BAND, high - low, CH), BF16) for (low, high), _, _ in PARTS],
             pltpu.VMEM((6, 3, 2, BAND), jnp.int32),
             pltpu.SMEM((6, 3, 2, BAND), jnp.int32),
+            pltpu.SMEM((2, 2 * BAND), jnp.int32),
+            pltpu.SMEM((2, 2 * BAND), F32),
             pltpu.VMEM((BAND, WIDTH, CH), BF16),
             pltpu.VMEM((BAND, WIDTH, CH), BF16),
             pltpu.VMEM((BAND + 16, CH, WIDTH), BF16),

time: 90.2 us -> 78 us (0.86)
  Pallas kernels: 88.4 us -> 76.4 us
    pallas_call x1, Pallas kernels: 88.4 us -> 76.4 us  [on_device(): pl.pallas_call(functools.partial(kernel, tiles), out_shape=jax.ShapeDtype...]
where the time goes in v2:
time: 78 us; the launch traced here: 77.8 us
  Pallas kernels  76.4 us (98%)
  local copies, waits for them, and re-layouts  1.38 us (2%)
    pallas_call x1, Pallas kernels, on_device(): pl.pallas_call(functools.partial(kernel, tiles), out_shape=jax.ShapeDtype...  76.4 us

profile of v2, /device:TPU:1, one launch (start us, length us, event | category | flops | bytes accessed | tf_op | source)
XLA Modules:
  0.0 77.8 jit_solution(2366003610431071149)
XLA Ops:
  0.0 76.4 %shard_map.127 = f32[1,2,32,128]{3,2,1,0:T(8,128)} custom-call(bf16[1,2,64,64,256]{4,3,2,1,0:T(8,128)(2,1)} %frames.1, bf16[576,128]{1,0:T(8,128)(2,1)} %bitcast.9, f32[1,128]{1,0:T(1,128)} %bitcast.15, s32[1,1,3,2,32]{4,3,2,1,0:T(2,128)} %sent.1, s32[1,1,2,64]{3,2,1,0:T(2,128)} %bitcast.11, f32[1,1,2,64]{3,2,1,0:T(2,128)} %bitcast.12, ...), custom_call_target="tpu_custom_call" | custom-call | tf_op jit(solution)/shard_map/pallas_call | solution.py:472
  76.4 1.4 %copy.15 = f32[1,2,32,128]{3,2,1,0:T(8,128)} copy(f32[1,2,32,128]{3,2,1,0:T(8,128)} %shard_map.127) | data formatting | bytes 65536

commit v3 on v2

--- a/solution.py
+++ b/solution.py
@@ -18,8 +18,6 @@
 MID = 192
 WIDTH = 128
 BAND = 32
-GROUP = 8
-GROUPS = 2 * BAND // GROUP
 SPAN = 9
 NT = (((1,), (1,)), ((), ()))
 TN = (((0,), (0,)), ((), ()))
@@ -29,6 +27,14 @@
     ((80, 128), (64, 128), (48, 128)),
 
 )
+
+
+UNITS = tuple(
+    (f * BAND + first, count)
+    for f in range(2)
+    for first, count in ((29, 3), (25, 4), (17, 8), (9, 8), (1, 8), (0, 1))
+)
+GROUPS = len(UNITS)
 
 
 def centre_of(step_row):
@@ -65,62 +71,36 @@
     split,
     taps,
     bias_t,
-    *rest,
+    *buffers,
 ):
-    rows, rest = rest[: len(PARTS)], rest[len(PARTS) :]
-    run(tiles, frames, feat_w, feat_b, sent, slots, blend, lanes, corr_w, corr_b, mid_w, mid_b,
-        flow_w, flow_b, out, xin, picks, conv_w, split, taps, bias_t, rows, *rest)
-
-
-def run(
-    tiles,
-    frames,
-    feat_w,
-    feat_b,
-    sent,
-    slots,
-    blend,
-    lanes,
-    corr_w,
-    corr_b,
-    mid_w,
-    mid_b,
-    flow_w,
-    flow_b,
-    out,
-    xin,
-    picks,
-    conv_w,
-    split,
-    taps,
-    bias_t,
-    rows,
-    table_v,
-    table_s,
-    row_of,
-    weight_of,
-    g0,
-    g1,
-    g1_t,
-    halo,
-    mirror,
-    packed,
-    corr_k,
-    tail,
-    hid,
-    mid_in,
-    mid_k,
-    in_sem,
-    halo_send,
-    halo_recv,
-    row_send,
-    row_recv,
-    table_send,
-    table_recv,
-    edge_send,
-    edge_recv,
-    local_sem,
-):
+    rows, buffers = buffers[: len(PARTS)], buffers[len(PARTS) :]
+    (
+        table_v,
+        table_s,
+        row_of,
+        weight_of,
+        g0,
+        g1,
+        g1_t,
+        halo,
+        mirror,
+        packed,
+        corr_k,
+        tail,
+        hid,
+        mid_in,
+        mid_k,
+        in_sem,
+        halo_send,
+        halo_recv,
+        row_send,
+        row_recv,
+        table_send,
+        table_recv,
+        edge_send,
+        edge_recv,
+        local_sem,
+    ) = buffers
     t = lax.axis_index("tiles")
     r = lax.axis_index("rows")
     right, left = lax.rem(t + 1, tiles), lax.rem(t + tiles - 1, tiles)
@@ -170,25 +150,22 @@
 
         lax.fori_loop(0, 16, regroup, 0, unroll=8)
 
-    def conv_group(f, g):
+    def conv_rows(f, y, count):
+        tiles_in = [taps[f, pl.ds(2 * (y + n), 3)].reshape(9 * CIN, WIDTH) for n in range(count)]
+        found = jnp.dot(conv_w[...], jnp.concatenate(tiles_in, axis=1), preferred_element_type=F32)
+        for n in range(count):
+            feature = found[:, n * WIDTH : (n + 1) * WIDTH] + bias_t[...]
+            feature = jnp.maximum(feature, 0.0).astype(BF16).T
+            for k in range(len(PARTS)):
+                low, high = PARTS[k][0]
+                rows[k][2 * BAND * (2 + r) + f * BAND + y + n] = feature[low:high]
+
+    def conv_pairs(f, y, pairs):
         def pair(p, carry):
-            y = 8 * g + 2 * p
-            upper = taps[f, pl.ds(2 * y, 3)].reshape(9 * CIN, WIDTH)
-            lower = taps[f, pl.ds(2 * y + 2, 3)].reshape(9 * CIN, WIDTH)
-            found = jnp.dot(
-                conv_w[...],
-                jnp.concatenate([upper, lower], axis=1),
-                preferred_element_type=F32,
-            )
-            for i in range(2):
-                feature = found[:, i * WIDTH : (i + 1) * WIDTH] + bias_t[...]
-                feature = jnp.maximum(feature, 0.0).astype(BF16).T
-                for k in range(len(PARTS)):
-                    low, high = PARTS[k][0]
-                    rows[k][2 * BAND * (2 + r) + f * BAND + y + i] = feature[low:high]
-            return carry
-
-        lax.fori_loop(0, 4, pair, 0, unroll=2)
+            conv_rows(f, y + 2 * p, 2)
+            return carry
+
+        lax.fori_loop(0, pairs, pair, 0, unroll=2)
 
     def remote(src, dst, send, recv, peer):
         return pltpu.make_async_remote_copy(
@@ -199,9 +176,10 @@
         window = 2 * (2, 0, 1, 2, 0)[kind] + r
         place = 2 * (1, 1, 1, 2, 0)[kind] + r
         peer = ((right, r), (left, r), (t, other), (t, other), (t, other))[kind]
+        first, count = UNITS[j]
         return remote(
-            rows[k].at[pl.ds(2 * BAND * place + GROUP * j, GROUP)],
-            rows[k].at[pl.ds(2 * BAND * window + GROUP * j, GROUP)],
+            rows[k].at[pl.ds(2 * BAND * place + first, count)],
+            rows[k].at[pl.ds(2 * BAND * window + first, count)],
             row_send.at[kind, k, j],
             row_recv.at[kind, k, j],
             peer,
@@ -217,26 +195,34 @@
         window = (4, 0, 2, 4, 0)[i] + r
         tables.append(remote(table_v.at[2 + r], table_v.at[window], table_send.at[i], table_recv.at[i], peer))
 
-    split_group(0, 3)
-    pl.semaphore_wait(barrier, 5)
+    def send(k, j):
+        for kind in range(3):
+            row_copy(kind, k, j).start()
+
     for f in range(2):
-        if f:
-            split_group(f, 3)
+        base = 6 * f
+        split_group(f, 3)
+        conv_rows(f, 31, 1)
+        conv_rows(f, 29, 2)
+        if f == 0:
+            pl.semaphore_wait(barrier, 5)
+        send(0, base)
         halos[f].start()
-        for g in (3, 2, 1, 0):
-            if g:
-                split_group(f, g - 1)
-            else:
-                halos[f].wait()
-                above = taps[f, 65]
-                taps[f, 0] = jnp.where(r == 0, jnp.zeros_like(above), above)
-            conv_group(f, g)
-            for kind in range(3):
-                row_copy(kind, 0, 4 * f + g).start()
+        conv_pairs(f, 25, 2)
+        send(0, base + 1)
+        for n, g in enumerate((2, 1, 0)):
+            split_group(f, g)
+            conv_pairs(f, 8 * g + 1, 4)
+            send(0, base + 2 + n)
+        halos[f].wait()
+        above = taps[f, 65]
+        taps[f, 0] = jnp.where(r == 0, jnp.zeros_like(above), above)
+        conv_rows(f, 0, 1)
+        send(0, base + 5)
         if f == 0:
             for copy in tables:
                 copy.start()
-    group_order = [4 * f + g for f, g in order]
+    group_order = range(GROUPS)
     for k in range(1, len(PARTS)):
         for j in group_order:
             for kind in range(3):
@@ -261,8 +247,7 @@
     lax.fori_loop(0, 8, clear_rim, 0)
     mid_load.wait()
     for tap in range(9):
-        a, b = tap // 3, tap % 3
-        mid_k[a, b * HID : (b + 1) * HID, :] = mid_in[tap].T
+        mid_k[tap * HID : (tap + 1) * HID, :] = mid_in[tap].T
 
     for copy in tables:
         copy.wait()
@@ -421,11 +406,10 @@
 
         def head(i, carry):
             y = 8 * lax.rem(i + r, 4)
-            total = None
-            for a in range(3):
-                part = hid[pl.ds(y + a, 8), m0:m1].reshape(8 * columns, 3 * HID)
-                term = jnp.dot(part, mid_k[a], preferred_element_type=F32)
-                total = term if total is None else total + term
+            part = jnp.concatenate(
+                [hid[pl.ds(y + a, 8), m0:m1].reshape(8 * columns, 3 * HID) for a in range(3)], axis=1
+            )
+            total = jnp.dot(part, mid_k[...], preferred_element_type=F32)
             middle = jnp.maximum(total + mid_b[...], 0.0).astype(BF16)
             flow = lax.dot_general(flow_w[...], middle, NT, preferred_element_type=F32)
             for c in range(2):
@@ -496,7 +480,7 @@
             pltpu.VMEM((BAND, 16, HID), F32),
             pltpu.VMEM((BAND + 2, WIDTH, 3 * HID), BF16),
             pltpu.VMEM((9, MID, HID), BF16),
-            pltpu.VMEM((3, 3 * HID, MID), BF16),
+            pltpu.VMEM((9 * HID, MID), BF16),
             dma((8,)),
             dma((2,)),
             dma((2,)),

time: 78 us -> 77.1 us (0.988)
  Pallas kernels: 76.4 us -> 75.5 us
    pallas_call x1, Pallas kernels: 76.4 us -> 75.5 us  [on_device(): pl.pallas_call(functools.partial(kernel, tiles), out_shape=jax.ShapeDtype...]
where the time goes in v3:
time: 77.1 us; the launch traced here: 76.9 us
  Pallas kernels  75.5 us (98%)
  local copies, waits for them, and re-layouts  1.38 us (2%)
    pallas_call x1, Pallas kernels, on_device(): pl.pallas_call(functools.partial(kernel, tiles), out_shape=jax.ShapeDtype...  75.5 us

profile of v3, /device:TPU:1, one launch (start us, length us, event | category | flops | bytes accessed | tf_op | source)
XLA Modules:
  0.0 76.9 jit_solution(13142060469868490514)
XLA Ops:
  0.0 75.5 %shard_map.127 = f32[1,2,32,128]{3,2,1,0:T(8,128)} custom-call(bf16[1,2,64,64,256]{4,3,2,1,0:T(8,128)(2,1)} %frames.1, bf16[576,128]{1,0:T(8,128)(2,1)} %bitcast.9, f32[1,128]{1,0:T(1,128)} %bitcast.15, s32[1,1,3,2,32]{4,3,2,1,0:T(2,128)} %sent.1, s32[1,1,2,64]{3,2,1,0:T(2,128)} %bitcast.11, f32[1,1,2,64]{3,2,1,0:T(2,128)} %bitcast.12, ...), custom_call_target="tpu_custom_call" | custom-call | tf_op jit(solution)/shard_map/pallas_call | solution.py:456
  75.5 1.4 %copy.15 = f32[1,2,32,128]{3,2,1,0:T(8,128)} copy(f32[1,2,32,128]{3,2,1,0:T(8,128)} %shard_map.127) | data formatting | bytes 65536

commit v4 on v3

--- a/solution.py
+++ b/solution.py
@@ -29,12 +29,15 @@
 )
 
 
-UNITS = tuple(
-    (f * BAND + first, count)
-    for f in range(2)
-    for first, count in ((29, 3), (25, 4), (17, 8), (9, 8), (1, 8), (0, 1))
+UNITS = (
+    tuple(
+        (f * BAND + first, count)
+        for f in range(2)
+        for first, count in ((29, 3), (25, 4), (17, 8), (9, 8), (1, 8), (0, 1))
+    ),
+    ((0, 16), (16, 16), (32, 16), (48, 8), (56, 8)),
 )
-GROUPS = len(UNITS)
+MOST = max(len(units) for units in UNITS)
 
 
 def centre_of(step_row):
@@ -176,7 +179,7 @@
         window = 2 * (2, 0, 1, 2, 0)[kind] + r
         place = 2 * (1, 1, 1, 2, 0)[kind] + r
         peer = ((right, r), (left, r), (t, other), (t, other), (t, other))[kind]
-        first, count = UNITS[j]
+        first, count = UNITS[k][j]
         return remote(
             rows[k].at[pl.ds(2 * BAND * place + first, count)],
             rows[k].at[pl.ds(2 * BAND * window + first, count)],
@@ -222,9 +225,8 @@
         if f == 0:
             for copy in tables:
                 copy.start()
-    group_order = range(GROUPS)
     for k in range(1, len(PARTS)):
-        for j in group_order:
+        for j in range(len(UNITS[k])):
             for kind in range(3):
                 row_copy(kind, k, j).start()
 
@@ -270,7 +272,7 @@
     place8 = lax.broadcasted_iota(jnp.int32, (8, WIDTH), 0)
 
     def forward(k):
-        for j in group_order:
+        for j in range(len(UNITS[k])):
             for kind in range(2):
                 row_copy(kind, k, j).wait_recv()
                 row_copy(3 + kind, k, j).start()
@@ -280,7 +282,7 @@
         width = c1 - c0
 
         forward(k)
-        for j in group_order:
+        for j in range(len(UNITS[k])):
             for kind in (2, 3, 4):
                 row_copy(kind, k, j).wait_recv()
 
@@ -358,7 +360,7 @@
                             )
             return carry
 
-        lax.fori_loop(0, 8, correlate, 0, unroll=2)
+        lax.fori_loop(0, 8, correlate, 0, unroll=4 if k else 1)
 
         kept = 16 if k else 0
         side = lax.broadcasted_iota(jnp.int32, (width + kept, HID), 0)
@@ -428,7 +430,7 @@
         do_part(k)
 
     for k in range(len(PARTS)):
-        for j in group_order:
+        for j in range(len(UNITS[k])):
             for kind in range(5):
                 row_copy(kind, k, j).wait_send()
 
@@ -484,8 +486,8 @@
             dma((8,)),
             dma((2,)),
             dma((2,)),
-            dma((5, parts, GROUPS)),
-            dma((5, parts, GROUPS)),
+            dma((5, parts, MOST)),
+            dma((5, parts, MOST)),
             dma((5,)),
             dma((5,)),
             dma((2, parts)),

time: 77.1 us -> 76.6 us (level)
  no operation moved by 1% of the time
where the time goes in v4:
time: 76.6 us; the launch traced here: 76.5 us
  Pallas kernels  75.1 us (98%)
  local copies, waits for them, and re-layouts  1.38 us (2%)
    pallas_call x1, Pallas kernels, on_device(): pl.pallas_call(functools.partial(kernel, tiles), out_shape=jax.ShapeDtype...  75.1 us

profile of v4, /device:TPU:1, one launch (start us, length us, event | category | flops | bytes accessed | tf_op | source)
XLA Modules:
  0.0 76.5 jit_solution(8770391973555274212)
XLA Ops:
  0.0 75.1 %shard_map.127 = f32[1,2,32,128]{3,2,1,0:T(8,128)} custom-call(bf16[1,2,64,64,256]{4,3,2,1,0:T(8,128)(2,1)} %frames.1, bf16[576,128]{1,0:T(8,128)(2,1)} %bitcast.9, f32[1,128]{1,0:T(1,128)} %bitcast.15, s32[1,1,3,2,32]{4,3,2,1,0:T(2,128)} %sent.1, s32[1,1,2,64]{3,2,1,0:T(2,128)} %bitcast.11, f32[1,1,2,64]{3,2,1,0:T(2,128)} %bitcast.12, ...), custom_call_target="tpu_custom_call" | custom-call | tf_op jit(solution)/shard_map/pallas_call | solution.py:458
  75.1 1.4 %copy.15 = f32[1,2,32,128]{3,2,1,0:T(8,128)} copy(f32[1,2,32,128]{3,2,1,0:T(8,128)} %shard_map.127) | data formatting | bytes 65536
